TPU v7x, 256 devices: a whole 4x4x8 slice. The times are simulated.
256 devices in a mesh: grp: 8 (over x_hi, y), row: 4 (over x_lo, core), col: 8 (over z).
Axes of the slice: x: 4 (x_hi: 2, x_lo: 2; x = x_hi * 2 + x_lo), y: 4, z: 8, core: 2. Of those that a mesh axis runs over, the one named last changes fastest.
Arguments:
- queries: bfloat16 [8192, 2560], P(('grp', 'col'), 'row'), may hold values from -70 to 70
- suffix_keys: bfloat16 [8192, 512], P(('grp', 'col'), 'row'), may hold values from -15 to 15
- suffix_values: bfloat16 [8192, 512], P(('grp', 'col'), 'row'), may hold values from -6 to 6
- prefix_keys: bfloat16 [8, 4096, 512], P('grp', 'col', 'row'), may hold values from -15 to 15
- prefix_values: bfloat16 [8, 4096, 512], P('grp', 'col', 'row'), may hold values from -6 to 6
- sink_logits: float32 [20], P('row'), may hold values from 0 to 14
- suffix_lengths: int32 [8, 4], P('grp'), may hold values from 1 to 512, 1024 in all within a row
- out_weight: bfloat16 [2560, 2560], P('row', 'col'), may hold values from -0.125 to 0.125
- residual: bfloat16 [8192, 2560], P(('grp', 'col'), 'row'), may hold values from -12 to 12
- norm_gain: float32 [2560], replicated, may hold values from 0.25 to 1.75
- expert_ids: int32 [8192, 6], P(('grp', 'col')), may hold values from 0 to 63, all different within a row; in each aligned block of 128 rows (0 to 127, 128 to 255, ...) at most 24 rows name the same one
- gate_fixed: int32 [8192, 6], P(('grp', 'col')), may hold values from 1 to 4095
- gate_weight: bfloat16 [64, 2560, 1536], P(('grp', 'col'), None, 'row'), may hold values from -0.125 to 0.125
- up_weight: bfloat16 [64, 2560, 1536], P(('grp', 'col'), None, 'row'), may hold values from -0.125 to 0.125
- down_weight: bfloat16 [64, 2560, 1536], P(('grp', 'col'), None, 'row'), may hold values from -0.15625 to 0.15625
Outputs:
- hidden_state: bfloat16 [8192, 2560], P(('grp', 'col'), 'row')
- expert_mix: bfloat16 [8192, 2560], P(('grp', 'col'), 'row')
Inputs may be any that keep to these rules, and one draw needn't show every extreme that they name: `suffix_lengths`: each row holds the suffix lengths of one group's 4 requests and sums to 1024; the largest of each row is 512. `expert_ids`: each token names 6 different experts. In each aligned block of 128 rows no expert is named by more than 24 rows, a bound that some block reaches.
All inputs are finite; a program needn't handle non-finite values.
Results may differ from a plain program's by a relative error of at most 0.014.
Values may be sent and summed in bfloat16 or wider, within the bound.
No kernel may reach another device: no remote copies, remote signals or barrier semaphores. Data moves between devices by JAX's collectives and lax.ppermute only.
A program may use at most 128 MiB of HBM per device.

v0:
```python
import jax
import jax.numpy as jnp
from jax import lax
from jax.sharding import PartitionSpec as P

HD = 128
TOPK = 6


eps = 1e-06


def segment_of(positions, lengths):
    ends = jnp.cumsum(lengths)
    return jnp.sum((positions[:, None] >= ends[None, :]).astype(jnp.int32), axis=1)


def normalize(rows, gain):
    values = rows.astype(jnp.float32)
    mean_square = jnp.mean(values * values, axis=-1, keepdims=True)
    return (values * lax.rsqrt(mean_square + eps) * gain).astype(jnp.bfloat16)


def local(
    queries,
    suffix_keys,
    suffix_values,
    prefix_keys,
    prefix_values,
    sink_logits,
    suffix_lengths,
    out_weight,
    residual,
    norm_gain,
    expert_ids,
    gate_fixed,
    gate_weight,
    up_weight,
    down_weight,
):
    tokens_here = queries.shape[0]
    query_heads = queries.shape[1] // HD
    kv_heads = suffix_keys.shape[1] // HD
    group_size = query_heads // kv_heads
    column = lax.axis_index("col")
    query_positions = column * tokens_here + jnp.arange(tokens_here, dtype=jnp.int32)
    lengths = suffix_lengths[0]
    query_segments = segment_of(query_positions, lengths)
    query_blocks = queries.reshape(tokens_here, kv_heads, group_size, HD)
    sink_rows = jnp.broadcast_to(
        sink_logits.reshape(kv_heads, group_size, 1), (kv_heads, group_size, tokens_here)
    )
    start_state = (
        sink_rows,
        jnp.ones_like(sink_rows),
        jnp.zeros((kv_heads, group_size, tokens_here, HD), jnp.float32),
    )

    def absorb(state, keys, values, visible):
        count = keys.shape[0]
        key_blocks = keys.reshape(count, kv_heads, HD)
        value_blocks = values.reshape(count, kv_heads, HD)
        scores = jnp.einsum(
            "tkgd,pkd->kgtp", query_blocks, key_blocks, preferred_element_type=jnp.float32
        ) * HD ** (-0.5)
        scores = jnp.where(visible[None, None], scores, -1e30)
        old_max, old_total, old_sum = state
        new_max = jnp.maximum(old_max, jnp.max(scores, axis=-1))
        weights = jnp.where(visible[None, None], jnp.exp(scores - new_max[..., None]), 0.0)
        factor = jnp.exp(old_max - new_max)
        new_total = old_total * factor + jnp.sum(weights, axis=-1)
        new_sum = old_sum * factor[..., None] + jnp.einsum(
            "kgtp,pkd->kgtd",
            weights.astype(jnp.bfloat16),
            value_blocks,
            preferred_element_type=jnp.float32,
        )
        return (new_max, new_total, new_sum)

    pieces = (
        lax.all_gather(prefix_keys[0], "col", axis=0, tiled=True),
        lax.all_gather(prefix_values[0], "col", axis=0, tiled=True),
    )
    visible = jnp.ones((tokens_here, pieces[0].shape[0]), dtype=bool)
    state = absorb(start_state, pieces[0], pieces[1], visible)
    pieces = (
        lax.all_gather(suffix_keys, "col", axis=0, tiled=True),
        lax.all_gather(suffix_values, "col", axis=0, tiled=True),
    )
    count = pieces[0].shape[0]
    key_positions = jnp.arange(count, dtype=jnp.int32)
    same_request = query_segments[:, None] == segment_of(key_positions, lengths)[None, :]
    visible = same_request & (key_positions[None, :] <= query_positions[:, None])
    state = absorb(state, pieces[0], pieces[1], visible)
    attended = (state[2] / state[1][..., None]).transpose(2, 0, 1, 3)
    attended = attended.reshape(tokens_here, query_heads * HD).astype(jnp.bfloat16)
    partial_rows = jnp.dot(
        attended,
        lax.all_gather(out_weight, "col", axis=1, tiled=True),
        preferred_element_type=jnp.float32,
    )
    projected = lax.psum_scatter(partial_rows, "row", scatter_dimension=1, tiled=True)
    hidden_state = (residual.astype(jnp.float32) + projected).astype(jnp.bfloat16)
    experts = lax.axis_size("grp") * lax.axis_size("col")
    capacity = max(2, min(tokens_here, 2 * tokens_here * TOPK // experts))
    width_here = hidden_state.shape[1]
    flat_experts = expert_ids.reshape(-1)
    selection = (flat_experts[:, None] == jnp.arange(experts, dtype=jnp.int32)[None, :]).astype(
        jnp.int32
    )
    slots = jnp.sum((jnp.cumsum(selection, axis=0) - selection) * selection, axis=1)
    outgoing = jnp.zeros((experts, capacity, width_here), jnp.bfloat16)
    outgoing = outgoing.at[flat_experts, slots].set(jnp.repeat(hidden_state, TOPK, axis=0))
    received = lax.all_to_all(outgoing, ("grp", "col"), split_axis=0, concat_axis=0, tiled=True)
    flat_rows = received.reshape(-1, width_here)
    whole_rows = lax.all_gather(flat_rows, "row", axis=1, tiled=True)
    normed = normalize(whole_rows, norm_gain)
    gate = jnp.dot(normed, gate_weight[0], preferred_element_type=jnp.float32)
    upper = jnp.dot(normed, up_weight[0], preferred_element_type=jnp.float32)
    active = (jax.nn.silu(gate) * upper).astype(jnp.bfloat16)
    terms = lax.dot_general(
        active, down_weight[0], (((1,), (1,)), ((), ())), preferred_element_type=jnp.float32
    )
    result_rows = lax.psum_scatter(terms, "row", scatter_dimension=1, tiled=True).astype(
        jnp.bfloat16
    )
    returned = lax.all_to_all(
        result_rows.reshape(received.shape), ("grp", "col"), split_axis=0, concat_axis=0, tiled=True
    )
    picked = returned[flat_experts, slots].reshape(tokens_here, TOPK, width_here)
    shares = gate_fixed.astype(jnp.float32)
    shares = shares / jnp.sum(shares, axis=1, keepdims=True)
    expert_mix = jnp.sum(picked.astype(jnp.float32) * shares[..., None], axis=1).astype(
        jnp.bfloat16
    )
    return (hidden_state, expert_mix)


def solution(mesh):
    placed = (
        P(("grp", "col"), "row"),
        P(("grp", "col"), "row"),
        P(("grp", "col"), "row"),
        P("grp", "col", "row"),
        P("grp", "col", "row"),
        P("row"),
        P("grp", None),
        P("row", "col"),
        P(("grp", "col"), "row"),
        P(),
        P(("grp", "col"), None),
        P(("grp", "col"), None),
        P(("grp", "col"), None, "row"),
        P(("grp", "col"), None, "row"),
        P(("grp", "col"), None, "row"),
    )
    return jax.shard_map(
        local,
        mesh=mesh,
        in_specs=placed,
        out_specs=(P(("grp", "col"), "row"), P(("grp", "col"), "row")),
        check_vma=False,
    )
```

profile of v0, /device:TPU:12, one launch (start us, length us, event | category | flops | bytes accessed | tf_op | source)
XLA Modules:
  0.0 659.1 jit_solution(12636515733742104376)
XLA Ops:
  7.2 0.7 all-gather.11.cloned.1.call-update
  8.0 1.7 copy.38
  9.7 0.7 all-gather.7.cloned.1.call-update
  10.4 1.1 copy.36
  11.5 0.9 copy.41
  12.4 0.8 reduce-window.18
  13.2 0.1 convert_reduce_fusion
  13.3 0.1 convert_reduce_fusion.2
  13.4 28.9 %all_gather.20 = bf16[1024,128]{1,0:T(8,128)(2,1)S(1)} all-gather(bf16[128,128]{1,0:T(8,128)(2,1)} %param.16), channel_id=1, replica_groups=mesh['grp'=8,'row'=4,'col'=8] {'col'}, dimensions={0}, use_global_device_ids=true | all-gather | bytes 294912 | tf_op jit(solution)/shard_map/all_gather | solution.py:87
  42.3 22.9 %all_gather.21 = bf16[1024,128]{0,1:T(8,128)(2,1)S(1)} all-gather(bf16[128,128]{0,1:T(8,128)(2,1)S(1)} %copy.41), channel_id=1, replica_groups=mesh['grp'=8,'row'=4,'col'=8] {'col'}, dimensions={0}, use_global_device_ids=true | all-gather | bytes 294912 | tf_op jit(solution)/shard_map/all_gather | solution.py:88
  65.2 0.2 fusion.46
  65.4 2.0 fusion.10
  67.4 2.9 bitcast_reduce_fusion
  70.4 0.6 fusion.21
  71.0 1.7 fusion.4
  72.7 1.5 copy-done.2
  74.3 0.8 fusion.24
  75.1 16.1 %all-gather.13.cloned.1.call-done = bf16[1,4096,128]{1,2,0:T(8,128)(2,1)} async-done(((bf16[1,512,128]{1,2,0:T(8,128)(2,1)}), bf16[1,4096,128]{1,2,0:T(8,128)(2,1)}) %all-gather.13.cloned.1.call-update) | async-done | bytes 1048592 | tf_op jit(solution)/shard_map/all_gather | solution.py:82
  91.2 6.3 fusion.40
  97.6 40.0 %all-gather.7.cloned.1.call-done = bf16[640,2560]{0,1:T(8,128)(2,1)} async-done(((bf16[640,320]{0,1:T(8,128)(2,1)}), bf16[640,2560]{0,1:T(8,128)(2,1)}) %all-gather.7.cloned.1.call-update) | async-done | bytes 3276816 | tf_op jit(solution)/shard_map/all_gather | solution.py:99
  137.6 4.2 fusion.63
  141.9 0.1 copy.43
  142.0 0.1 eq.49
  142.1 0.1 eq.45
  142.2 0.1 reshape.370
  142.4 1.8 reduce-window.19
  144.2 0.3 slice_reduce_fusion
  144.5 0.1 fusion.52
  144.7 20.0 %reduce-scatter.3.cloned.1.call-done = f32[128,640]{1,0:T(8,128)} async-done(((f32[128,2560]{1,0:T(8,128)}), f32[128,640]{1,0:T(8,128)}) %reduce-scatter.3.cloned.1.call-update) | async-done | bytes 327696 | tf_op jit(solution)/shard_map/reduce_scatter | solution.py:102
  164.7 1.0 add_convert_fusion
  165.7 0.2 broadcast_in_dim.44
  165.8 1.2 reshape.384
  167.0 1.4 broadcast_in_dim.43
  168.5 98.6 %scatter_fusion = bf16[64,24,640]{2,1,0:T(8,128)(2,1)} fusion(bf16[64,24,640]{2,1,0:T(8,128)(2,1)} %broadcast_in_dim.43, s32[768]{0:T(1024)S(1)} %get-tuple-element.3, bf16[768,640]{1,0:T(8,128)(2,1)S(1)} %copy-done.5), kind=kCustom, calls=%fused_computation.1 | custom fusion | bytes 2955264 | tf_op jit(solution)/shard_map/scatter | solution.py:113
  267.1 60.7 %all_to_all.10 = bf16[64,24,640]{2,1,0:T(8,128)(2,1)} all-to-all(bf16[64,24,640]{2,1,0:T(8,128)(2,1)} %scatter_fusion), channel_id=1, replica_groups=mesh['grp'=8,'row'=4,'col'=8] {'grp','col'}, dimensions={0} | all-to-all | bytes 3932160 | tf_op jit(solution)/shard_map/all_to_all | solution.py:114
  327.9 75.1 %all-gather.9.cloned.1.call-done = bf16[1536,2560]{1,0:T(8,128)(2,1)} async-done(((bf16[1536,640]{1,0:T(8,128)(2,1)}), bf16[1536,2560]{1,0:T(8,128)(2,1)}) %all-gather.9.cloned.1.call-update) | async-done | bytes 7864336 | tf_op jit(solution)/shard_map/all_gather | solution.py:116
  403.0 5.0 fusion
  408.0 0.5 copy-done.4
  408.5 7.4 %fusion.12 = f32[1536,384]{1,0:T(8,128)} fusion(bf16[1536,2560]{1,0:T(8,128)(2,1)S(1)} %copy-done.4, f32[2560]{0:T(1024)S(1)} %copy-done.11, f32[1536]{0:T(1024)S(1)} %add_rsqrt_fusion, bf16[1,2560,384]{2,1,0:T(8,128)(2,1)} %param.27), kind=kOutput, calls=%fused_computation.20 | convolution fusion | flops 3035627520 | bytes 12206080 | tf_op jit(solution)/shard_map/dot_general | solution.py:118
  415.9 15.1 %fusion.15 = f32[1536,2560]{1,0:T(8,128)} fusion(f32[1536,384]{1,0:T(8,128)} %fusion.12, bf16[1536,2560]{1,0:T(8,128)(2,1)} %all-gather.9.cloned.1.call-done, f32[2560]{0:T(1024)S(1)} %copy-done.11, f32[1536]{0:T(1024)S(1)} %add_rsqrt_fusion, bf16[1,2560,384]{2,1,0:T(8,128)(2,1)S(1)} %copy-done, bf16[1,2560,384]{2,1,0:T(8,128)(2,1)} %param.28), kind=kOutput, calls=%fused_computation.21 | convolution fusion | flops 6059065344 | bytes 29900800 | tf_op jit(solution)/shard_map/dot_general | solution.py:121
  431.0 143.3 %reduce-scatter.5.cloned.1.call-done = f32[1536,640]{1,0:T(8,128)} async-done(((f32[1536,2560]{1,0:T(8,128)}), f32[1536,640]{1,0:T(8,128)}) %reduce-scatter.5.cloned.1.call-update) | async-done | bytes 3932176 | tf_op jit(solution)/shard_map/reduce_scatter | solution.py:124
  574.3 3.6 convert_element_type.76
  577.9 13.4 %all-to-all-start.1 = ((bf16[64,24,640]{2,1,0:T(8,128)(2,1)}), bf16[64,24,640]{2,1,0:T(8,128)(2,1)}, u32[]{:S(2)}, u32[]{:S(2)}) async-start(bf16[64,24,640]{2,1,0:T(8,128)(2,1)} %bitcast.24), calls=%async_computation.3 | async-start | bytes 3932160 | tf_op jit(solution)/shard_map/all_to_all | solution.py:127
  591.4 0.1 copy.47
  591.5 47.3 %all-to-all-done.1 = bf16[64,24,640]{2,1,0:T(8,128)(2,1)} async-done(((bf16[64,24,640]{2,1,0:T(8,128)(2,1)}), bf16[64,24,640]{2,1,0:T(8,128)(2,1)}, u32[]{:S(2)}, u32[]{:S(2)}) %all-to-all-start.1) | async-done | bytes 1966112 | tf_op jit(solution)/shard_map/all_to_all | solution.py:127
  638.8 8.5 %gather_fusion = bf16[768,640]{1,0:T(8,128)(2,1)S(1)} fusion(bf16[64,24,640]{2,1,0:T(8,128)(2,1)} %all-to-all-done.1, s32[768]{0:T(1024)S(1)} %get-tuple-element.2), kind=kCustom, calls=%fused_computation | custom fusion | bytes 1972224 | tf_op jit(solution)/shard_map/gather | solution.py:130
  647.3 1.6 reshape.375
  649.0 3.3 multiply_reduce_fusion
  (43 shorter events, 0.7 us)
Async XLA Ops:
  7.2 408.7 %copy-start = (bf16[1,2560,384]{2,1,0:T(8,128)(2,1)S(1)}, bf16[1,2560,384]{2,1,0:T(8,128)(2,1)}, u32[]{:S(2)}) copy-start(bf16[1,2560,384]{2,1,0:T(8,128)(2,1)} %param.29) | copy-start | bytes 5898244
  7.2 60.2 %all-gather.11.cloned.1.call-start = ((), (), s32[]{:S(2)}) async-start(), calls=%async_computation.8 | async-start | bytes 1179648 | tf_op jit(solution)/shard_map/all_gather | solution.py:81
  7.9 83.3 %all-gather.13.cloned.1.call-start = ((), (), s32[]{:S(2)}) async-start(), calls=%async_computation.9 | async-start | bytes 1179648 | tf_op jit(solution)/shard_map/all_gather | solution.py:82
  9.7 127.9 %all-gather.7.cloned.1.call-start = ((), (), s32[]{:S(2)}) async-start(), calls=%async_computation.4 | async-start | bytes 3686400 | tf_op jit(solution)/shard_map/all_gather | solution.py:99
  10.4 154.3 %reduce-scatter.3.cloned.1.call-start = ((), (), s32[]{:S(2)}) async-start(), calls=%async_computation.5 | async-start | bytes 1638400 | tf_op jit(solution)/shard_map/reduce_scatter | solution.py:102
  67.4 2.9 copy-start.10
  67.4 3.0 copy-start.3
  70.3 4.0 copy-start.2
  137.5 4.3 copy-start.9
  137.6 27.1 %copy-start.7 = (bf16[128,640]{1,0:T(8,128)(2,1)S(1)}, bf16[128,640]{1,0:T(8,128)(2,1)}, u32[]{:S(2)}) copy-start(bf16[128,640]{1,0:T(8,128)(2,1)} %param.23) | copy-start | bytes 491524
  141.8 261.2 %all-gather.9.cloned.1.call-start = ((), (), s32[]{:S(2)}) async-start(), calls=%async_computation.6 | async-start | bytes 9830400 | tf_op jit(solution)/shard_map/all_gather | solution.py:116
  165.7 2.8 copy-start.6
  167.0 1.5 copy-start.5
  327.9 80.1 %copy-start.11 = (f32[2560]{0:T(1024)S(1)}, f32[2560]{0:T(1024)}, u32[]{:S(2)}) copy-start(f32[2560]{0:T(1024)} %param.24) | copy-start | bytes 30724
  327.9 246.4 %reduce-scatter.5.cloned.1.call-start = ((), (), s32[]{:S(2)}) async-start(), calls=%async_computation.7 | async-start | bytes 19660800 | tf_op jit(solution)/shard_map/reduce_scatter | solution.py:124
  403.0 5.5 copy-start.4
  577.9 13.4 %copy-start.8 = (s32[128,6]{0,1:T(8,128)S(1)}, s32[128,6]{0,1:T(8,128)}, u32[]{:S(2)}) copy-start(s32[128,6]{0,1:T(8,128)} %param.26) | copy-start | bytes 9220
  577.9 60.9 %all-to-all-start.1 = ((bf16[64,24,640]{2,1,0:T(8,128)(2,1)}), bf16[64,24,640]{2,1,0:T(8,128)(2,1)}, u32[]{:S(2)}, u32[]{:S(2)}) async-start(bf16[64,24,640]{2,1,0:T(8,128)(2,1)} %bitcast.24), calls=%async_computation.3 | async-start | bytes 3932160 | tf_op jit(solution)/shard_map/all_to_all | solution.py:127
  638.8 13.4 %copy-start.1 = (bf16[1,2560,384]{2,1,0:T(8,128)(2,1)S(1)}, bf16[1,2560,384]{2,1,0:T(8,128)(2,1)}, u32[]{:S(2)}) copy-start(bf16[1,2560,384]{2,1,0:T(8,128)(2,1)} %param.29) | copy-start | bytes 5898244
Sparse Core Ops, SparseCore 0:
  9.8 41.9 all-gather.10
  54.1 37.0 all-gather.12
  93.0 44.4 all-gather.6
  141.9 22.6 reduce-scatter.2
  328.0 74.9 all-gather.8
  431.2 143.1 reduce-scatter.4
where the time goes:
time: 665 us; the launch traced here: 659 us
  waiting for transfers between devices  343 us (52%)
  local copies, waits for them, and re-layouts  118 us (18%)
  blocking collectives  112 us (17%)
  matrix products  38.8 us (6%)
  other arithmetic  18.6 us (3%)
  between operations  14.3 us (2%)
  starting transfers between devices  13.6 us (2%)
    reduce_scatter x1, waiting for transfers between devices, local(): lax.psum_scatter(terms, 'row', scatter_dimension=1, tiled=True)  143 us
    scatter x1, local copies, waits for them, and re-layouts, local(): outgoing.at[flat_experts, slots].set(jnp.repeat(hidden_state, TOPK, axis=0))  98.6 us
    all_gather x1, waiting for transfers between devices, local(): whole_rows = lax.all_gather(flat_rows, 'row', axis=1, tiled=True)  75.1 us
    all_to_all x1, blocking collectives, local(): lax.all_to_all(outgoing, ('grp', 'col'), split_axis=0, concat_axis=0, til...  60.7 us
    all_to_all x1, waiting for transfers between devices, local(): lax.all_to_all(result_rows.reshape(received.shape), ('grp', 'col'), split...  47.3 us
    all_gather x1, waiting for transfers between devices, local(): lax.all_gather(out_weight, 'col', axis=1, tiled=True)  40 us
    all_gather x1, blocking collectives, local(): lax.all_gather(suffix_keys, 'col', axis=0, tiled=True)  28.9 us
    all_gather x1, blocking collectives, local(): lax.all_gather(suffix_values, 'col', axis=0, tiled=True)  22.9 us
  transfers between devices with their start and end apart: 7, of which 6 were waited for; matrix products, arithmetic and copies ran while one was open for 3% of the time, Pallas kernels for 0%

commit v1 on v0

v1 whole, which is shorter than its diff:
```python
import functools

import jax
import jax.numpy as jnp
from jax import lax
from jax.experimental import pallas as pl
from jax.experimental.pallas import tpu as pltpu
from jax.sharding import PartitionSpec as P

HD = 128
TOPK = 6
CAP = 24
CHUNKS = 1
PAD = 16
eps = 1e-06
BF = jnp.bfloat16
F32 = jnp.float32
VMEM = pl.BlockSpec(memory_space=pltpu.VMEM)
SMEM = pl.BlockSpec(memory_space=pltpu.SMEM)
PARAMS = pltpu.CompilerParams(vmem_limit_bytes=56 * 1024 * 1024)


def matmul_t(a, b):
    return lax.dot_general(a, b, (((1,), (1,)), ((), ())), preferred_element_type=F32)


def attend_kernel(first, last, offsets, ring, info_ref, sink_ref, q_ref, *refs):
    split = last
    count = 2 if split else len(offsets)
    blocks, refs = refs[:count], refs[count:]
    tokens = q_ref.shape[0]
    heads = q_ref.shape[1] // HD
    rows = tokens * heads
    q = jnp.concatenate([q_ref[:, h * HD : (h + 1) * HD] for h in range(heads)], axis=0)
    if first:
        top = jnp.concatenate(
            [jnp.full((tokens, 1), sink_ref[h], F32) for h in range(heads)], axis=0
        )
        total = jnp.ones((rows, 1), F32)
        acc = jnp.zeros((rows, HD), F32)
    else:
        top, total, acc = refs[0][:, :1], refs[1][:, :1], refs[2][...]
        refs = refs[3:]
    z = info_ref[4]
    token = lax.rem(lax.broadcasted_iota(jnp.int32, (rows, 1), 0), tokens)
    q_pos = z * tokens + token
    begin = jnp.zeros_like(q_pos)
    for i in range(4):
        end = info_ref[i]
        begin = jnp.maximum(begin, jnp.where(q_pos >= end, end, 0))
    for i, offset in enumerate(offsets):
        if split:
            keys, values = blocks[0][...], blocks[1][...]
        else:
            half = blocks[i].shape[0] // 2
            keys, values = blocks[i][:half], blocks[i][half:]
        shared = keys.shape[0] - tokens
        scores = matmul_t(q, keys) * HD ** (-0.5)
        source = lax.rem(z - offset + ring, ring)
        k_pos = source * tokens + lax.broadcasted_iota(jnp.int32, (1, tokens), 1)
        visible = (k_pos >= begin) & (k_pos <= q_pos)
        scores = jnp.concatenate(
            [scores[:, :shared], jnp.where(visible, scores[:, shared:], -1e30)], axis=1
        )
        new_top = jnp.maximum(top, jnp.max(scores, axis=1, keepdims=True))
        weights = jnp.exp(scores - new_top)
        factor = jnp.exp(top - new_top)
        total = total * factor + jnp.sum(weights, axis=1, keepdims=True)
        acc = acc * factor + jnp.dot(weights.astype(BF), values, preferred_element_type=F32)
        top = new_top
    if last:
        out = (acc / total).astype(BF)
        for h in range(heads):
            refs[0][:, h * HD : (h + 1) * HD] = out[h * tokens : (h + 1) * tokens]
    else:
        refs[0][...] = jnp.broadcast_to(top, (rows, HD))
        refs[1][...] = jnp.broadcast_to(total, (rows, HD))
        refs[2][...] = acc


def attend(info, sinks, queries, state, blocks, offsets, ring, last):
    tokens = queries.shape[0]
    rows = tokens * (queries.shape[1] // HD)
    first = state is None
    state = () if first else tuple(state)
    if last:
        out_shape = jax.ShapeDtypeStruct(queries.shape, BF)
        out_specs = VMEM
    else:
        out_shape = (jax.ShapeDtypeStruct((rows, HD), F32),) * 3
        out_specs = (VMEM,) * 3
    return pl.pallas_call(
        functools.partial(attend_kernel, first, last, tuple(offsets), ring),
        out_shape=out_shape,
        in_specs=[SMEM, SMEM] + [VMEM] * (1 + len(blocks) + len(state)),
        out_specs=out_specs,
        compiler_params=PARAMS,
        name="attend",
    )(info, sinks, queries, *blocks, *state)


def project_kernel(stride, r_ref, a_ref, w_ref, own_ref, across_ref, pair_ref):
    r = r_ref[0]
    width = own_ref.shape[1] // 2
    a = a_ref[...]
    for j in range(4):
        for half in range(2):
            block = (r ^ j) * 2 + half
            w = w_ref[pl.ds(pl.multiple_of(block * stride, 16), width), :]
            part = matmul_t(a, w)
            cols = slice(half * width, (half + 1) * width)
            if j == 0:
                own_ref[:, cols] = part
            elif j == 2:
                across_ref[:, cols] = part
            else:
                pair_ref[j // 2, :, cols] = part.astype(BF)


def project(r, attended, gathered, stride):
    tokens = attended.shape[0]
    width = 2 * (stride - PAD)
    return pl.pallas_call(
        functools.partial(project_kernel, stride),
        out_shape=(
            jax.ShapeDtypeStruct((tokens, width), F32),
            jax.ShapeDtypeStruct((tokens, width), F32),
            jax.ShapeDtypeStruct((2, tokens, width), BF),
        ),
        in_specs=[SMEM, VMEM, VMEM],
        out_specs=(VMEM, VMEM, VMEM),
        compiler_params=PARAMS,
        name="project",
    )(r, attended, gathered)


def routing(ids, z, ring):
    tokens = ids.shape[1]
    experts = (lax.broadcasted_iota(jnp.int32, (8, tokens), 0) * ring + z).astype(F32)
    hits = [(ids[k : k + 1] == experts).astype(F32) for k in range(TOPK)]
    chosen = sum(hits)
    before = (
        lax.broadcasted_iota(jnp.int32, (tokens, tokens), 0)
        < lax.broadcasted_iota(jnp.int32, (tokens, tokens), 1)
    ).astype(BF)
    slot = jnp.dot(chosen.astype(BF), before, preferred_element_type=F32)
    slot = jnp.where(chosen > 0, slot, -1.0)
    place = lax.broadcasted_iota(jnp.int32, (8, CAP, tokens), 1).astype(F32)
    picks = (place == slot[:, None, :]).astype(F32)
    return hits, picks


def table_of(ex_ref, source):
    return ex_ref[source, :, :].astype(F32)


def select_kernel(offsets, ring, z_ref, ex_ref, *refs):
    z = z_ref[0]
    out_ref = refs[-1]
    for i, offset in enumerate(offsets):
        table = table_of(ex_ref, lax.rem(z - offset + ring, ring))
        tokens = refs[i].shape[0]
        _, picks = routing(table[:TOPK, :tokens], z, ring)
        picks = picks.reshape(8 * CAP, tokens).astype(BF)
        rows = jnp.dot(picks, refs[i][...], preferred_element_type=F32).astype(BF)
        for g in range(8):
            out_ref[g, i * CAP : (i + 1) * CAP, :] = rows[g * CAP : (g + 1) * CAP]


def select(z, extras, blocks, offsets, ring):
    width = blocks[0].shape[1]
    return pl.pallas_call(
        functools.partial(select_kernel, tuple(offsets), ring),
        out_shape=jax.ShapeDtypeStruct((8, CAP * len(blocks), width), BF),
        in_specs=[SMEM, VMEM] + [VMEM] * len(blocks),
        out_specs=VMEM,
        compiler_params=PARAMS,
        name="select",
    )(z, extras, *blocks)


def combine_kernel(offsets, ring, z_ref, ex_ref, ret_ref, out_ref):
    z = z_ref[0]
    tokens = out_ref.shape[1]
    for i, offset in enumerate(offsets):
        table = table_of(ex_ref, lax.rem(z - offset + ring, ring))
        hits, picks = routing(table[:TOPK, :tokens], z, ring)
        gates = 64.0 * table[:TOPK, tokens : 2 * tokens] + table[:TOPK, 2 * tokens : 3 * tokens]
        shares = gates / jnp.sum(gates, axis=0, keepdims=True)
        mine = sum(hits[k] * shares[k : k + 1] for k in range(TOPK))
        weights = (picks * mine[:, None, :]).reshape(8 * CAP, tokens)
        high = weights.astype(BF)
        low = (weights - high.astype(F32)).astype(BF)
        rows = jnp.concatenate([ret_ref[g, i * CAP : (i + 1) * CAP, :] for g in range(8)], axis=0)
        dims = (((0,), (0,)), ((), ()))
        out_ref[i] = lax.dot_general(
            high, rows, dims, preferred_element_type=F32
        ) + lax.dot_general(low, rows, dims, preferred_element_type=F32)


def combine(z, extras, returned, offsets, ring, tokens):
    width = returned.shape[2]
    return pl.pallas_call(
        functools.partial(combine_kernel, tuple(offsets), ring),
        out_shape=jax.ShapeDtypeStruct((len(offsets), tokens, width), F32),
        in_specs=[SMEM, VMEM, VMEM],
        out_specs=VMEM,
        compiler_params=PARAMS,
        name="combine",
    )(z, extras, returned)


def ffn_kernel(r_ref, gain_ref, wg_ref, wu_ref, wd_ref, x0, x1, x2, x3, o0, o13, o2):
    r = r_ref[0]
    parts = [x[...].astype(F32) for x in (x0, x1, x2, x3)]
    width = parts[0].shape[1]
    square = sum(jnp.sum(p * p, axis=1, keepdims=True) for p in parts)
    scale = lax.rsqrt(square * (1.0 / (4 * width)) + eps)
    gate, upper = 0.0, 0.0
    for j in range(4):
        at = pl.ds(pl.multiple_of((r ^ j) * width, 128), width)
        normed = (parts[j] * scale * gain_ref[pl.ds(r ^ j, 1), :]).astype(BF)
        gate = gate + jnp.dot(normed, wg_ref[at, :], preferred_element_type=F32)
        upper = upper + jnp.dot(normed, wu_ref[at, :], preferred_element_type=F32)
    active = (gate / (1.0 + jnp.exp(-gate)) * upper).astype(BF)
    for j in range(4):
        at = pl.ds(pl.multiple_of((r ^ j) * width, 128), width)
        terms = matmul_t(active, wd_ref[at, :]).astype(BF)
        if j == 0:
            o0[...] = terms
        elif j == 2:
            o2[...] = terms
        else:
            o13[j // 2] = terms


def ffn(r, gain, wg, wu, wd, parts):
    rows, width = parts[0].shape
    step = 256 if rows % 256 == 0 else 192
    whole = pl.BlockSpec(wg.shape, lambda i: (0, 0))
    tile = pl.BlockSpec((step, width), lambda i: (i, 0))
    return pl.pallas_call(
        ffn_kernel,
        grid=(rows // step,),
        out_shape=(
            jax.ShapeDtypeStruct((rows, width), BF),
            jax.ShapeDtypeStruct((2, rows, width), BF),
            jax.ShapeDtypeStruct((rows, width), BF),
        ),
        in_specs=[SMEM, pl.BlockSpec(gain.shape, lambda i: (0, 0)), whole, whole, whole] + [tile] * 4,
        out_specs=(tile, pl.BlockSpec((2, step, width), lambda i: (0, i, 0)), tile),
        compiler_params=PARAMS,
        name="ffn",
    )(r, gain, wg, wu, wd, *parts)


def local(
    queries,
    suffix_keys,
    suffix_values,
    prefix_keys,
    prefix_values,
    sink_logits,
    suffix_lengths,
    out_weight,
    residual,
    norm_gain,
    expert_ids,
    gate_fixed,
    gate_weight,
    up_weight,
    down_weight,
):
    tokens = queries.shape[0]
    ring = lax.axis_size("col")
    rows4 = lax.axis_size("row")
    z = lax.axis_index("col").astype(jnp.int32)
    z1 = z.reshape(1)
    r1 = lax.axis_index("row").astype(jnp.int32).reshape(1)
    ends = jnp.cumsum(suffix_lengths[0]).astype(jnp.int32)
    info = jnp.concatenate([ends, z1])

    def shift(x, k):
        return lax.ppermute(x, "col", [(i, (i + k) % ring) for i in range(ring)])

    def swap(x, k):
        return lax.ppermute(x, "row", [(i, i ^ k) for i in range(rows4)])

    def both_ways(own, low, high):
        found = {0: own}
        up, down = own, own
        for k in range(1, 4):
            up, down = shift(up, 1), shift(down, -1)
            found[k], found[-k] = up, down
        found[4] = (shift(low(up), 1), shift(high(down), -1))
        return found

    half = prefix_keys.shape[1] + tokens
    kv = jnp.concatenate([prefix_keys[0], suffix_keys, prefix_values[0], suffix_values], axis=0)
    found = both_ways(kv, lambda x: x[:half], lambda x: x[half:])
    gates = gate_fixed.T
    table = jnp.concatenate([expert_ids.T, gates // 64, gates % 64], axis=1).astype(BF)
    columns, features = out_weight.shape[1], out_weight.shape[0]
    table = jnp.pad(table, ((0, PAD - TOPK), (0, features - table.shape[1])))
    gathered = lax.all_gather(
        jnp.concatenate([out_weight.T, table], axis=0), "col", axis=0, tiled=True
    )
    stride = columns + PAD
    extras = gathered.reshape(ring, stride, features)[:, columns:, : 3 * tokens]

    sinks = sink_logits
    state = attend(
        info, sinks, queries, None, [found[k] for k in (0, 1, -1)], (0, 1, -1), ring, False
    )
    for k in (2, 3):
        state = attend(
            info, sinks, queries, state, [found[k], found[-k]], (k, -k), ring, False
        )
    attended = attend(info, sinks, queries, state, found[4], (4,), ring, True)
    own, across, pair = project(r1, attended, gathered, stride)
    pair = swap(pair, 1).astype(F32)
    across = swap((across + pair[1]).astype(BF), 2).astype(F32)
    hidden = (residual.astype(F32) + (own + pair[0] + across)).astype(BF)

    middle = tokens // 2
    found = both_ways(hidden, lambda x: x[:middle], lambda x: x[middle:])
    found[4] = jnp.concatenate(found[4], axis=0)
    order = (0, 1, -1, 2, -2, 3, -3, 4)
    size = len(order) // CHUNKS
    gain = norm_gain.reshape(rows4, -1)
    width = hidden.shape[1]
    sums = {}
    for c in range(CHUNKS):
        offsets = order[c * size : (c + 1) * size]
        outgoing = select(z1, extras, [found[k] for k in offsets], offsets, ring)
        received = lax.all_to_all(outgoing, "grp", split_axis=0, concat_axis=0, tiled=True)
        x0 = received.reshape(-1, width)
        x2 = swap(x0, 2)
        x1 = swap(x0, 1)
        x3 = swap(x2, 1)
        o0, o13, o2 = ffn(r1, gain, gate_weight[0], up_weight[0], down_weight[0], (x0, x1, x2, x3))
        k13 = swap(o13, 1).astype(F32)
        far = swap((o2.astype(F32) + k13[1]).astype(BF), 2)
        result = (o0.astype(F32) + k13[0] + far.astype(F32)).astype(BF)
        returned = lax.all_to_all(
            result.reshape(outgoing.shape), "grp", split_axis=0, concat_axis=0, tiled=True
        )
        mixed = combine(z1, extras, returned, offsets, ring, tokens)
        for i, k in enumerate(offsets):
            sums[k] = mixed[i]

    low = shift(sums[4][:middle].astype(BF), -1).astype(F32)
    high = shift(sums[4][middle:].astype(BF), 1).astype(F32)
    down = sums[3] + jnp.pad(low, ((0, middle), (0, 0)))
    up = sums[-3] + jnp.pad(high, ((middle, 0), (0, 0)))
    for k in (2, 1, 0):
        down = shift(down.astype(BF), -1).astype(F32)
        up = shift(up.astype(BF), 1).astype(F32)
        if k:
            down = sums[k] + down
            up = sums[-k] + up
    expert_mix = (sums[0] + down + up).astype(BF)
    return (hidden, expert_mix)


def solution(mesh):
    placed = (
        P(("grp", "col"), "row"),
        P(("grp", "col"), "row"),
        P(("grp", "col"), "row"),
        P("grp", "col", "row"),
        P("grp", "col", "row"),
        P("row"),
        P("grp", None),
        P("row", "col"),
        P(("grp", "col"), "row"),
        P(),
        P(("grp", "col"), None),
        P(("grp", "col"), None),
        P(("grp", "col"), None, "row"),
        P(("grp", "col"), None, "row"),
        P(("grp", "col"), None, "row"),
    )
    return jax.shard_map(
        local,
        mesh=mesh,
        in_specs=placed,
        out_specs=(P(("grp", "col"), "row"), P(("grp", "col"), "row")),
        check_vma=False,
    )
```

time: 665 us -> 372 us (0.56)
  waiting for transfers between devices: 343 us -> 183 us
  local copies, waits for them, and re-layouts: 118 us -> 3 us
  blocking collectives: 112 us -> 57.4 us
  Pallas kernels: 0 us -> 54.2 us
  matrix products: 38.8 us -> 0 us
  starting transfers between devices: 13.6 us -> 42.1 us
    ppermute x0 -> x31, waiting for transfers between devices: none -> 183 us  [the longest x7 101 us: swap(): return lax.ppermute(x, 'row', [(i, i ^ k) for i in range(rows4)])]
    reduce_scatter x2 -> x0, waiting for transfers between devices: 163 us -> none  [the longest x1 143 us: local(): lax.psum_scatter(terms, 'row', scatter_dimension=1, tiled=True)]
    all_gather x4 -> x1, waiting for transfers between devices: 131 us -> 0.01 us  [local(): lax.all_gather(jnp.concatenate([out_weight.T, table], axis=0), 'col', axi...]
    scatter x1 -> x0, local copies, waits for them, and re-layouts: 98.6 us -> none  [local(): outgoing.at[flat_experts, slots].set(jnp.repeat(hidden_state, TOPK, axis=0))]
    pallas_call x0 -> x8, Pallas kernels: none -> 54.2 us  [the longest x1 22.5 us: ffn(): pl.pallas_call(ffn_kernel, grid=(rows // step,), out_shape=(jax.ShapeDtyp...]
    all_gather x2 -> x0, blocking collectives: 51.8 us -> none  [the longest x1 28.9 us: local(): lax.all_gather(suffix_keys, 'col', axis=0, tiled=True)]
    all_to_all x1 -> x0, waiting for transfers between devices: 47.3 us -> none  [local(): lax.all_to_all(result_rows.reshape(received.shape), ('grp', 'col'), split...]
    ppermute x0 -> x31, starting transfers between devices: none -> 42 us  [the longest x24 39 us: shift(): return lax.ppermute(x, 'col', [(i, (i + k) % ring) for i in range(ring)])]
  transfers between devices with their start and end apart: 7 -> 32, of which waited for: 6 -> 25; matrix products, arithmetic and copies ran while one was open for 3% -> 1% of each run, Pallas kernels for 0% -> 5%
where the time goes in v1:
time: 372 us; the launch traced here: 367 us
  waiting for transfers between devices  183 us (49%)
  blocking collectives  57.4 us (15%)
  Pallas kernels  54.2 us (15%)
  starting transfers between devices  42.1 us (11%)
  between operations  14.8 us (4%)
  other arithmetic  12.5 us (3%)
    ppermute x7, waiting for transfers between devices, swap(): return lax.ppermute(x, 'row', [(i, i ^ k) for i in range(rows4)])  101 us
    ppermute x24, waiting for transfers between devices, shift(): return lax.ppermute(x, 'col', [(i, (i + k) % ring) for i in range(ring)])  82.3 us
    ppermute x24, starting transfers between devices, shift(): return lax.ppermute(x, 'col', [(i, (i + k) % ring) for i in range(ring)])  39 us
    all_to_all x1, blocking collectives, local(): lax.all_to_all(result.reshape(outgoing.shape), 'grp', split_axis=0, conca...  30 us
    all_to_all x1, blocking collectives, local(): lax.all_to_all(outgoing, 'grp', split_axis=0, concat_axis=0, tiled=True)  27.4 us
    pallas_call x1, Pallas kernels, ffn(): pl.pallas_call(ffn_kernel, grid=(rows // step,), out_shape=(jax.ShapeDtyp...  22.5 us
    pallas_call x4, Pallas kernels, attend(): pl.pallas_call(functools.partial(attend_kernel, first, last, tuple(offset...  17.7 us
  transfers between devices with their start and end apart: 32, of which 25 were waited for; matrix products, arithmetic and copies ran while one was open for 1% of the time, Pallas kernels for 5%

profile of v1, /device:TPU:12, one launch (start us, length us, event | category | flops | bytes accessed | tf_op | source)
XLA Modules:
  0.0 367.0 jit_solution(3058222615075127727)
XLA Ops:
  8.6 1.8 pad_maximum_fusion
  10.5 1.0 pad_maximum_fusion.1.refs_0_
  11.5 5.9 %collective-permute-start.4 = (bf16[1280,128]{1,0:T(8,128)(2,1)S(1)}, bf16[1280,128]{1,0:T(8,128)(2,1)S(1)}, u32[]{:S(2)}, u32[]{:S(2)}) collective-permute-start(bf16[1280,128]{1,0:T(8,128)(2,1)S(1)} %pad_maximum_fusion.1.refs_0_), channel_id=1, source_target_pairs={{0,7},{1,0},{2,1},{3,2},{4,3},{5,4},{6,5},{7,6},{8,15},{9,8},{10,9... | collective-permute-start | bytes 983048 | tf_op jit(solution)/shard_map/ppermute | solution.py:284
  17.4 7.0 %collective-permute-done.4.refs_2_ = bf16[1280,128]{1,0:T(8,128)(2,1)S(1)} collective-permute-done((bf16[1280,128]{1,0:T(8,128)(2,1)S(1)}, bf16[1280,128]{1,0:T(8,128)(2,1)S(1)}, u32[]{:S(2)}, u32[]{:S(2)}) %collective-permute-start.4) | collective-permute-done | bytes 327712 | tf_op jit(solution)/shard_map/ppermute | solution.py:284
  24.4 3.7 %collective-permute-start.5 = (bf16[1280,128]{1,0:T(8,128)(2,1)S(1)}, bf16[1280,128]{1,0:T(8,128)(2,1)S(1)}, u32[]{:S(2)}, u32[]{:S(2)}) collective-permute-start(bf16[1280,128]{1,0:T(8,128)(2,1)S(1)} %collective-permute-done.4.refs_2_), channel_id=1, source_target_pairs={{0,7},{1,0},{2,1},{3,2},{4,3},{5,4},{6,5},{7,6},{8,15},{9,8},{10,9... | collective-permute-start | bytes 983048 | tf_op jit(solution)/shard_map/ppermute | solution.py:284
  28.1 14.3 %collective-permute-done.5.refs_1_ = bf16[1280,128]{1,0:T(8,128)(2,1)S(1)} collective-permute-done((bf16[1280,128]{1,0:T(8,128)(2,1)S(1)}, bf16[1280,128]{1,0:T(8,128)(2,1)S(1)}, u32[]{:S(2)}, u32[]{:S(2)}) %collective-permute-start.5) | collective-permute-done | bytes 327712 | tf_op jit(solution)/shard_map/ppermute | solution.py:284
  42.4 3.7 %collective-permute-start.6 = (bf16[1280,128]{1,0:T(8,128)(2,1)S(1)}, bf16[1280,128]{1,0:T(8,128)(2,1)S(1)}, u32[]{:S(2)}, u32[]{:S(2)}) collective-permute-start(bf16[1280,128]{1,0:T(8,128)(2,1)S(1)} %collective-permute-done.5.refs_1_), channel_id=1, source_target_pairs={{0,7},{1,0},{2,1},{3,2},{4,3},{5,4},{6,5},{7,6},{8,15},{9,8},{10,9... | collective-permute-start | bytes 983048 | tf_op jit(solution)/shard_map/ppermute | solution.py:284
  46.2 13.6 %collective-permute-done.6.refs_1_ = bf16[1280,128]{1,0:T(8,128)(2,1)S(1)} collective-permute-done((bf16[1280,128]{1,0:T(8,128)(2,1)S(1)}, bf16[1280,128]{1,0:T(8,128)(2,1)S(1)}, u32[]{:S(2)}, u32[]{:S(2)}) %collective-permute-start.6) | collective-permute-done | bytes 327712 | tf_op jit(solution)/shard_map/ppermute | solution.py:284
  59.9 3.8 %collective-permute-start.7 = (bf16[640,128]{1,0:T(8,128)(2,1)S(1)}, bf16[640,128]{1,0:T(8,128)(2,1)S(1)}, u32[]{:S(2)}, u32[]{:S(2)}) collective-permute-start(bf16[640,128]{1,0:T(8,128)(2,1)S(1)} %slice.80), channel_id=1, source_target_pairs={{0,7},{1,0},{2,1},{3,2},{4,3},{5,4},{6,5},{7,6},{8,15},{9,8},{10,9... | collective-permute-start | bytes 491528 | tf_op jit(solution)/shard_map/ppermute | solution.py:284
  65.2 5.2 %attend.4 = (f32[640,128]{1,0:T(8,128)}, f32[640,128]{1,0:T(8,128)}, f32[640,128]{1,0:T(8,128)}) custom-call(s32[5]{0:T(128)} %pad_add_fusion.info_ref, f32[5]{0:T(128)} %sink_ref.7, bf16[128,640]{1,0:T(8,128)(2,1)} %q_ref.7, bf16[1280,128]{1,0:T(8,128)(2,1)} %copy-done.4, bf16[1280,128]{1,0:T(8,128)(2,1)} %copy-done.11, bf16[1280,128]{1,0:T(8,128)(2,1)} %copy-done.10), custom_call_target="tpu_custom_call" | custom-call | tf_op jit(solution)/shard_map/attend/pallas_call | solution.py:92
  70.4 4.5 %attend.5 = (f32[640,128]{1,0:T(8,128)}, f32[640,128]{1,0:T(8,128)}, f32[640,128]{1,0:T(8,128)}) custom-call(s32[5]{0:T(128)} %pad_add_fusion.info_ref, f32[5]{0:T(128)} %sink_ref.7, bf16[128,640]{1,0:T(8,128)(2,1)} %q_ref.7, bf16[1280,128]{1,0:T(8,128)(2,1)} %copy-done.13, bf16[1280,128]{1,0:T(8,128)(2,1)} %copy-done.12, ...), custom_call_target="tpu_custom_call" | custom-call | tf_op jit(solution)/shard_map/attend/pallas_call | solution.py:92
  74.9 4.5 %attend.6 = (f32[640,128]{1,0:T(8,128)}, f32[640,128]{1,0:T(8,128)}, f32[640,128]{1,0:T(8,128)}) custom-call(s32[5]{0:T(128)} %pad_add_fusion.info_ref, f32[5]{0:T(128)} %sink_ref.7, bf16[128,640]{1,0:T(8,128)(2,1)} %q_ref.7, bf16[1280,128]{1,0:T(8,128)(2,1)} %copy-done.6, bf16[1280,128]{1,0:T(8,128)(2,1)} %copy-done.5, ...), custom_call_target="tpu_custom_call" | custom-call | tf_op jit(solution)/shard_map/attend/pallas_call | solution.py:92
  80.2 3.4 attend.7.a_ref
  83.6 4.2 %project.1 = (f32[128,640]{1,0:T(8,128)}, f32[128,640]{1,0:T(8,128)}, bf16[2,128,640]{2,1,0:T(8,128)(2,1)}) custom-call(s32[1]{0:T(128)} %bitcast.r_ref, bf16[128,640]{1,0:T(8,128)(2,1)} %attend.7.a_ref, bf16[2688,640]{1,0:T(8,128)(2,1)} %all-gather.2.cloned.1.call-done.w_ref), custom_call_target="tpu_custom_call" | custom-call | tf_op jit(solution)/shard_map/project/pallas_call | solution.py:123
  87.8 1.8 collective-permute-done.8
  89.7 1.0 fusion.21
  90.7 1.3 collective-permute-start.9
  92.0 5.0 %collective-permute-done.9 = bf16[128,640]{1,0:T(8,128)(2,1)S(1)} collective-permute-done((bf16[128,640]{1,0:T(8,128)(2,1)S(1)}, bf16[128,640]{1,0:T(8,128)(2,1)S(1)}, u32[]{:S(2)}, u32[]{:S(2)}) %collective-permute-start.9) | collective-permute-done | bytes 163872 | tf_op jit(solution)/shard_map/ppermute | solution.py:287
  97.0 1.0 fusion.25.refs_0_
  98.1 3.3 collective-permute-start.11
  101.5 2.7 collective-permute-done.11.refs_2_
  104.2 3.7 %collective-permute-start.13 = (bf16[128,640]{1,0:T(8,128)(2,1)S(1)}, bf16[128,640]{1,0:T(8,128)(2,1)S(1)}, u32[]{:S(2)}, u32[]{:S(2)}) collective-permute-start(bf16[128,640]{1,0:T(8,128)(2,1)S(1)} %collective-permute-done.11.refs_2_), channel_id=1, source_target_pairs={{0,7},{1,0},{2,1},{3,2},{4,3},{5,4},{6,5},{7,6},{8,15},{9,8},{10,9... | collective-permute-start | bytes 491528 | tf_op jit(solution)/shard_map/ppermute | solution.py:284
  108.1 2.7 collective-permute-done.13.refs_4_
  110.8 3.7 %collective-permute-start.15 = (bf16[128,640]{1,0:T(8,128)(2,1)S(1)}, bf16[128,640]{1,0:T(8,128)(2,1)S(1)}, u32[]{:S(2)}, u32[]{:S(2)}) collective-permute-start(bf16[128,640]{1,0:T(8,128)(2,1)S(1)} %collective-permute-done.13.refs_4_), channel_id=1, source_target_pairs={{0,7},{1,0},{2,1},{3,2},{4,3},{5,4},{6,5},{7,6},{8,15},{9,8},{10,9... | collective-permute-start | bytes 491528 | tf_op jit(solution)/shard_map/ppermute | solution.py:284
  114.6 2.7 collective-permute-done.15.refs_6_
  117.3 3.8 %collective-permute-start.17 = (bf16[64,640]{1,0:T(8,128)(2,1)S(1)}, bf16[64,640]{1,0:T(8,128)(2,1)S(1)}, u32[]{:S(2)}, u32[]{:S(2)}) collective-permute-start(bf16[64,640]{1,0:T(8,128)(2,1)S(1)} %slice.85), channel_id=1, source_target_pairs={{0,7},{1,0},{2,1},{3,2},{4,3},{5,4},{6,5},{7,6},{8,15},{9,8},{10,9... | collective-permute-start | bytes 245768 | tf_op jit(solution)/shard_map/ppermute | solution.py:284
  121.5 1.6 slice.83.ex_ref
  123.1 4.0 %collective-permute-done.16 = bf16[64,640]{1,0:T(8,128)(2,1)S(1)} collective-permute-done((bf16[64,640]{1,0:T(8,128)(2,1)S(1)}, bf16[64,640]{1,0:T(8,128)(2,1)S(1)}, u32[]{:S(2)}, u32[]{:S(2)}) %collective-permute-start.16) | collective-permute-done | bytes 81952 | tf_op jit(solution)/shard_map/ppermute | solution.py:284
  127.9 4.4 %select.36 = bf16[8,192,640]{2,1,0:T(8,128)(2,1)} custom-call(s32[1]{0:T(128)} %bitcast.3.z_ref, bf16[8,16,384]{2,1,0:T(8,128)(2,1)} %slice.83.ex_ref, bf16[128,640]{1,0:T(8,128)(2,1)} %copy-done.7, bf16[128,640]{1,0:T(8,128)(2,1)} %copy-done.15, bf16[128,640]{1,0:T(8,128)(2,1)} %copy-done.14, bf16[128,640]{1,0:T(8,128)(2,1)} %copy-done.17, ...), custom_call_target="tpu_custom_call" | custom-call | tf_op jit(solution)/shard_map/select/pallas_call | solution.py:172
  132.3 27.4 %all_to_all.10 = bf16[8,192,640]{2,1,0:T(8,128)(2,1)S(1)} all-to-all(bf16[8,192,640]{2,1,0:T(8,128)(2,1)} %select.36), channel_id=1, replica_groups=mesh['grp'=8,'row'=4,'col'=8] {'grp'}, dimensions={0} | all-to-all | bytes 3932160 | tf_op jit(solution)/shard_map/all_to_all | solution.py:336
  160.0 39.4 %collective-permute-done.19.x2 = bf16[1536,640]{1,0:T(8,128)(2,1)} collective-permute-done((bf16[1536,640]{1,0:T(8,128)(2,1)S(1)}, bf16[1536,640]{1,0:T(8,128)(2,1)}, u32[]{:S(2)}, u32[]{:S(2)}) %collective-permute-start.19) | collective-permute-done | bytes 1966112 | tf_op jit(solution)/shard_map/ppermute | solution.py:287
  200.0 3.7 %collective-permute-done.20.x3 = bf16[1536,640]{1,0:T(8,128)(2,1)} collective-permute-done((bf16[1536,640]{1,0:T(8,128)(2,1)}, bf16[1536,640]{1,0:T(8,128)(2,1)}, u32[]{:S(2)}, u32[]{:S(2)}) %collective-permute-start.20) | collective-permute-done | bytes 1966112 | tf_op jit(solution)/shard_map/ppermute | solution.py:287
  203.7 22.5 %ffn.1 = (bf16[1536,640]{1,0:T(8,128)(2,1)}, bf16[2,1536,640]{2,1,0:T(8,128)(2,1)}, bf16[1536,640]{1,0:T(8,128)(2,1)}) custom-call(s32[1]{0:T(128)} %bitcast.r_ref, f32[4,640]{1,0:T(4,128)} %reshape.58.gain_ref, bf16[2560,384]{1,0:T(8,128)(2,1)} %bitcast.124, bf16[2560,384]{1,0:T(8,128)(2,1)} %bitcast.125, bf16[2560,384]{1,0:T(8,128)(2,1)} %bitcast.126, ...), custom_call_target="tpu_custom_call" | custom-call | tf_op jit(solution)/shard_map/ffn/pallas_call | solution.py:242
  226.4 6.9 %collective-permute-done.21 = bf16[2,1536,640]{2,1,0:T(8,128)(2,1)S(1)} collective-permute-done((bf16[2,1536,640]{2,1,0:T(8,128)(2,1)}, bf16[2,1536,640]{2,1,0:T(8,128)(2,1)S(1)}, u32[]{:S(2)}, u32[]{:S(2)}) %collective-permute-start.21) | collective-permute-done | bytes 3932192 | tf_op jit(solution)/shard_map/ppermute | solution.py:287
  234.3 1.2 collective-permute-start.22
  235.4 44.0 %collective-permute-done.22 = bf16[1536,640]{1,0:T(8,128)(2,1)S(1)} collective-permute-done((bf16[1536,640]{1,0:T(8,128)(2,1)S(1)}, bf16[1536,640]{1,0:T(8,128)(2,1)S(1)}, u32[]{:S(2)}, u32[]{:S(2)}) %collective-permute-start.22) | collective-permute-done | bytes 1966112 | tf_op jit(solution)/shard_map/ppermute | solution.py:287
  280.2 30.0 %all_to_all.11.ret_ref = bf16[8,192,640]{2,1,0:T(8,128)(2,1)} all-to-all(bf16[8,192,640]{2,1,0:T(8,128)(2,1)S(1)} %bitcast.119), channel_id=1, replica_groups=mesh['grp'=8,'row'=4,'col'=8] {'grp'}, dimensions={0} | all-to-all | bytes 3932160 | tf_op jit(solution)/shard_map/all_to_all | solution.py:345
  310.2 5.5 %combine.1 = f32[8,128,640]{2,1,0:T(8,128)} custom-call(s32[1]{0:T(128)} %bitcast.3.z_ref, bf16[8,16,384]{2,1,0:T(8,128)(2,1)} %slice.83.ex_ref, bf16[8,192,640]{2,1,0:T(8,128)(2,1)} %all_to_all.11.ret_ref), custom_call_target="tpu_custom_call" | custom-call | tf_op jit(solution)/shard_map/combine/pallas_call | solution.py:203
  315.7 2.0 convert.21
  317.9 4.4 %collective-permute-done.23 = bf16[64,640]{1,0:T(8,128)(2,1)S(1)} collective-permute-done((bf16[64,640]{1,0:T(8,128)(2,1)S(1)}, bf16[64,640]{1,0:T(8,128)(2,1)S(1)}, u32[]{:S(2)}, u32[]{:S(2)}) %collective-permute-start.23) | collective-permute-done | bytes 81952 | tf_op jit(solution)/shard_map/ppermute | solution.py:284
  322.3 1.3 collective-permute-start.24
  323.6 4.7 %collective-permute-done.24 = bf16[128,640]{1,0:T(8,128)(2,1)S(1)} collective-permute-done((bf16[128,640]{1,0:T(8,128)(2,1)S(1)}, bf16[128,640]{1,0:T(8,128)(2,1)S(1)}, u32[]{:S(2)}, u32[]{:S(2)}) %collective-permute-start.24) | collective-permute-done | bytes 163872 | tf_op jit(solution)/shard_map/ppermute | solution.py:284
  328.4 1.9 collective-permute-start.25
  330.5 6.0 %collective-permute-done.27 = bf16[64,640]{1,0:T(8,128)(2,1)S(1)} collective-permute-done((bf16[64,640]{1,0:T(8,128)(2,1)S(1)}, bf16[64,640]{1,0:T(8,128)(2,1)S(1)}, u32[]{:S(2)}, u32[]{:S(2)}) %collective-permute-start.27) | collective-permute-done | bytes 81952 | tf_op jit(solution)/shard_map/ppermute | solution.py:284
  336.6 8.2 %collective-permute-done.28 = bf16[128,640]{1,0:T(8,128)(2,1)S(1)} collective-permute-done((bf16[128,640]{1,0:T(8,128)(2,1)S(1)}, bf16[128,640]{1,0:T(8,128)(2,1)S(1)}, u32[]{:S(2)}, u32[]{:S(2)}) %collective-permute-start.28) | collective-permute-done | bytes 163872 | tf_op jit(solution)/shard_map/ppermute | solution.py:284
  344.9 3.2 collective-permute-start.26
  348.2 4.2 %collective-permute-done.29 = bf16[128,640]{1,0:T(8,128)(2,1)S(1)} collective-permute-done((bf16[128,640]{1,0:T(8,128)(2,1)S(1)}, bf16[128,640]{1,0:T(8,128)(2,1)S(1)}, u32[]{:S(2)}, u32[]{:S(2)}) %collective-permute-start.29) | collective-permute-done | bytes 163872 | tf_op jit(solution)/shard_map/ppermute | solution.py:284
  352.5 6.5 %collective-permute-done.30 = bf16[128,640]{1,0:T(8,128)(2,1)S(1)} collective-permute-done((bf16[128,640]{1,0:T(8,128)(2,1)S(1)}, bf16[128,640]{1,0:T(8,128)(2,1)S(1)}, u32[]{:S(2)}, u32[]{:S(2)}) %collective-permute-start.30) | collective-permute-done | bytes 163872 | tf_op jit(solution)/shard_map/ppermute | solution.py:284
  (101 shorter events, 10.0 us)
Async XLA Ops:
  7.2 57.2 %copy-start.22 = (s32[1,4]{1,0:T(1,128)S(1)}, s32[1,4]{1,0:T(1,128)}, u32[]{:S(2)}) copy-start(s32[1,4]{1,0:T(1,128)} %param.21) | copy-start | bytes 52
  7.2 76.4 %all-gather.2.cloned.1.call-start = ((), (), s32[]{:S(2)}) async-start(), calls=%async_computation.2 | async-start | bytes 3870720 | tf_op jit(solution)/shard_map/all_gather | solution.py:305
  11.5 53.7 %copy-start.4 = (bf16[1280,128]{1,0:T(8,128)(2,1)}, bf16[1280,128]{1,0:T(8,128)(2,1)S(1)}, u32[]{:S(2)}) copy-start(bf16[1280,128]{1,0:T(8,128)(2,1)S(1)} %pad_maximum_fusion.1.refs_0_) | copy-start | bytes 983044
  11.5 12.9 %collective-permute-start.4 = (bf16[1280,128]{1,0:T(8,128)(2,1)S(1)}, bf16[1280,128]{1,0:T(8,128)(2,1)S(1)}, u32[]{:S(2)}, u32[]{:S(2)}) collective-permute-start(bf16[1280,128]{1,0:T(8,128)(2,1)S(1)} %pad_maximum_fusion.1.refs_0_), channel_id=1, source_target_pairs={{0,7},{1,0},{2,1},{3,2},{4,3},{5,4},{6,5},{7,6},{8,15},{9,8},{10,9... | collective-permute-start | bytes 983048 | tf_op jit(solution)/shard_map/ppermute | solution.py:284
  17.4 10.7 %collective-permute-start = (bf16[1280,128]{1,0:T(8,128)(2,1)S(1)}, bf16[1280,128]{1,0:T(8,128)(2,1)S(1)}, u32[]{:S(2)}, u32[]{:S(2)}) collective-permute-start(bf16[1280,128]{1,0:T(8,128)(2,1)S(1)} %pad_maximum_fusion.1.refs_0_), channel_id=1, source_target_pairs={{0,1},{1,2},{2,3},{3,4},{4,5},{5,6},{6,7},{7,0},{8,9},{9,10},{10,1... | collective-permute-start | bytes 983048 | tf_op jit(solution)/shard_map/ppermute | solution.py:284
  24.4 40.8 %copy-start.10 = (bf16[1280,128]{1,0:T(8,128)(2,1)}, bf16[1280,128]{1,0:T(8,128)(2,1)S(1)}, u32[]{:S(2)}) copy-start(bf16[1280,128]{1,0:T(8,128)(2,1)S(1)} %collective-permute-done.4.refs_2_) | copy-start | bytes 983044
  24.4 18.0 %collective-permute-start.5 = (bf16[1280,128]{1,0:T(8,128)(2,1)S(1)}, bf16[1280,128]{1,0:T(8,128)(2,1)S(1)}, u32[]{:S(2)}, u32[]{:S(2)}) collective-permute-start(bf16[1280,128]{1,0:T(8,128)(2,1)S(1)} %collective-permute-done.4.refs_2_), channel_id=1, source_target_pairs={{0,7},{1,0},{2,1},{3,2},{4,3},{5,4},{6,5},{7,6},{8,15},{9,8},{10,9... | collective-permute-start | bytes 983048 | tf_op jit(solution)/shard_map/ppermute | solution.py:284
  28.1 37.1 %copy-start.11 = (bf16[1280,128]{1,0:T(8,128)(2,1)}, bf16[1280,128]{1,0:T(8,128)(2,1)S(1)}, u32[]{:S(2)}) copy-start(bf16[1280,128]{1,0:T(8,128)(2,1)S(1)} %collective-permute-done.refs_1_) | copy-start | bytes 983044
  28.1 18.1 %collective-permute-start.1 = (bf16[1280,128]{1,0:T(8,128)(2,1)S(1)}, bf16[1280,128]{1,0:T(8,128)(2,1)S(1)}, u32[]{:S(2)}, u32[]{:S(2)}) collective-permute-start(bf16[1280,128]{1,0:T(8,128)(2,1)S(1)} %collective-permute-done.refs_1_), channel_id=1, source_target_pairs={{0,1},{1,2},{2,3},{3,4},{4,5},{5,6},{6,7},{7,0},{8,9},{9,10},{10,1... | collective-permute-start | bytes 983048 | tf_op jit(solution)/shard_map/ppermute | solution.py:284
  42.4 28.0 %copy-start.12 = (bf16[1280,128]{1,0:T(8,128)(2,1)}, bf16[1280,128]{1,0:T(8,128)(2,1)S(1)}, u32[]{:S(2)}) copy-start(bf16[1280,128]{1,0:T(8,128)(2,1)S(1)} %collective-permute-done.5.refs_1_) | copy-start | bytes 983044
  42.4 17.5 %collective-permute-start.6 = (bf16[1280,128]{1,0:T(8,128)(2,1)S(1)}, bf16[1280,128]{1,0:T(8,128)(2,1)S(1)}, u32[]{:S(2)}, u32[]{:S(2)}) collective-permute-start(bf16[1280,128]{1,0:T(8,128)(2,1)S(1)} %collective-permute-done.5.refs_1_), channel_id=1, source_target_pairs={{0,7},{1,0},{2,1},{3,2},{4,3},{5,4},{6,5},{7,6},{8,15},{9,8},{10,9... | collective-permute-start | bytes 983048 | tf_op jit(solution)/shard_map/ppermute | solution.py:284
  46.2 24.2 %copy-start.13 = (bf16[1280,128]{1,0:T(8,128)(2,1)}, bf16[1280,128]{1,0:T(8,128)(2,1)S(1)}, u32[]{:S(2)}) copy-start(bf16[1280,128]{1,0:T(8,128)(2,1)S(1)} %collective-permute-done.1.refs_0_) | copy-start | bytes 983044
  46.2 17.9 %collective-permute-start.2 = (bf16[1280,128]{1,0:T(8,128)(2,1)S(1)}, bf16[1280,128]{1,0:T(8,128)(2,1)S(1)}, u32[]{:S(2)}, u32[]{:S(2)}) collective-permute-start(bf16[1280,128]{1,0:T(8,128)(2,1)S(1)} %collective-permute-done.1.refs_0_), channel_id=1, source_target_pairs={{0,1},{1,2},{2,3},{3,4},{4,5},{5,6},{6,7},{7,0},{8,9},{9,10},{10,1... | collective-permute-start | bytes 983048 | tf_op jit(solution)/shard_map/ppermute | solution.py:284
  59.9 15.1 %copy-start.5 = (bf16[1280,128]{1,0:T(8,128)(2,1)}, bf16[1280,128]{1,0:T(8,128)(2,1)S(1)}, u32[]{:S(2)}) copy-start(bf16[1280,128]{1,0:T(8,128)(2,1)S(1)} %collective-permute-done.6.refs_1_) | copy-start | bytes 983044
  59.9 19.6 %collective-permute-start.7 = (bf16[640,128]{1,0:T(8,128)(2,1)S(1)}, bf16[640,128]{1,0:T(8,128)(2,1)S(1)}, u32[]{:S(2)}, u32[]{:S(2)}) collective-permute-start(bf16[640,128]{1,0:T(8,128)(2,1)S(1)} %slice.80), channel_id=1, source_target_pairs={{0,7},{1,0},{2,1},{3,2},{4,3},{5,4},{6,5},{7,6},{8,15},{9,8},{10,9... | collective-permute-start | bytes 491528 | tf_op jit(solution)/shard_map/ppermute | solution.py:284
  64.1 15.3 %collective-permute-start.3 = (bf16[640,128]{1,0:T(8,128)(2,1)S(1)}, bf16[640,128]{1,0:T(8,128)(2,1)S(1)}, u32[]{:S(2)}, u32[]{:S(2)}) collective-permute-start(bf16[640,128]{1,0:T(8,128)(2,1)S(1)} %slice.79), channel_id=1, source_target_pairs={{0,1},{1,2},{2,3},{3,4},{4,5},{5,6},{6,7},{7,0},{8,9},{9,10},{10,1... | collective-permute-start | bytes 491528 | tf_op jit(solution)/shard_map/ppermute | solution.py:284
  83.6 13.4 %copy-start.18 = (bf16[128,640]{1,0:T(8,128)(2,1)S(1)}, bf16[128,640]{1,0:T(8,128)(2,1)}, u32[]{:S(2)}) copy-start(bf16[128,640]{1,0:T(8,128)(2,1)} %param.23) | copy-start | bytes 491524
  87.8 1.8 collective-permute-start.8
  90.7 6.3 %collective-permute-start.9 = (bf16[128,640]{1,0:T(8,128)(2,1)S(1)}, bf16[128,640]{1,0:T(8,128)(2,1)S(1)}, u32[]{:S(2)}, u32[]{:S(2)}) collective-permute-start(bf16[128,640]{1,0:T(8,128)(2,1)S(1)} %fusion.21), channel_id=1, source_target_pairs={{0,16},{8,24},{16,0},{24,8},{1,17},{9,25},{17,1},{25,9},{2,18},{10... | collective-permute-start | bytes 491528 | tf_op jit(solution)/shard_map/ppermute | solution.py:287
  98.1 29.8 %copy-start.7 = (bf16[128,640]{1,0:T(8,128)(2,1)}, bf16[128,640]{1,0:T(8,128)(2,1)S(1)}, u32[]{:S(2)}) copy-start(bf16[128,640]{1,0:T(8,128)(2,1)S(1)} %fusion.25.refs_0_) | copy-start | bytes 491524
  98.1 6.2 %collective-permute-start.11 = (bf16[128,640]{1,0:T(8,128)(2,1)S(1)}, bf16[128,640]{1,0:T(8,128)(2,1)S(1)}, u32[]{:S(2)}, u32[]{:S(2)}) collective-permute-start(bf16[128,640]{1,0:T(8,128)(2,1)S(1)} %fusion.25.refs_0_), channel_id=1, source_target_pairs={{0,7},{1,0},{2,1},{3,2},{4,3},{5,4},{6,5},{7,6},{8,15},{9,8},{10,9... | collective-permute-start | bytes 491528 | tf_op jit(solution)/shard_map/ppermute | solution.py:284
  101.3 6.7 %collective-permute-start.10 = (bf16[128,640]{1,0:T(8,128)(2,1)S(1)}, bf16[128,640]{1,0:T(8,128)(2,1)S(1)}, u32[]{:S(2)}, u32[]{:S(2)}) collective-permute-start(bf16[128,640]{1,0:T(8,128)(2,1)S(1)} %fusion.25.refs_0_), channel_id=1, source_target_pairs={{0,1},{1,2},{2,3},{3,4},{4,5},{5,6},{6,7},{7,0},{8,9},{9,10},{10,1... | collective-permute-start | bytes 491528 | tf_op jit(solution)/shard_map/ppermute | solution.py:284
  104.2 23.6 %copy-start.14 = (bf16[128,640]{1,0:T(8,128)(2,1)}, bf16[128,640]{1,0:T(8,128)(2,1)S(1)}, u32[]{:S(2)}) copy-start(bf16[128,640]{1,0:T(8,128)(2,1)S(1)} %collective-permute-done.11.refs_2_) | copy-start | bytes 491524
  104.2 6.5 %collective-permute-start.13 = (bf16[128,640]{1,0:T(8,128)(2,1)S(1)}, bf16[128,640]{1,0:T(8,128)(2,1)S(1)}, u32[]{:S(2)}, u32[]{:S(2)}) collective-permute-start(bf16[128,640]{1,0:T(8,128)(2,1)S(1)} %collective-permute-done.11.refs_2_), channel_id=1, source_target_pairs={{0,7},{1,0},{2,1},{3,2},{4,3},{5,4},{6,5},{7,6},{8,15},{9,8},{10,9... | collective-permute-start | bytes 491528 | tf_op jit(solution)/shard_map/ppermute | solution.py:284
  108.1 19.8 %copy-start.15 = (bf16[128,640]{1,0:T(8,128)(2,1)}, bf16[128,640]{1,0:T(8,128)(2,1)S(1)}, u32[]{:S(2)}) copy-start(bf16[128,640]{1,0:T(8,128)(2,1)S(1)} %collective-permute-done.10.refs_1_) | copy-start | bytes 491524
  108.1 6.5 %collective-permute-start.12 = (bf16[128,640]{1,0:T(8,128)(2,1)S(1)}, bf16[128,640]{1,0:T(8,128)(2,1)S(1)}, u32[]{:S(2)}, u32[]{:S(2)}) collective-permute-start(bf16[128,640]{1,0:T(8,128)(2,1)S(1)} %collective-permute-done.10.refs_1_), channel_id=1, source_target_pairs={{0,1},{1,2},{2,3},{3,4},{4,5},{5,6},{6,7},{7,0},{8,9},{9,10},{10,1... | collective-permute-start | bytes 491528 | tf_op jit(solution)/shard_map/ppermute | solution.py:284
  110.8 17.1 %copy-start.16 = (bf16[128,640]{1,0:T(8,128)(2,1)}, bf16[128,640]{1,0:T(8,128)(2,1)S(1)}, u32[]{:S(2)}) copy-start(bf16[128,640]{1,0:T(8,128)(2,1)S(1)} %collective-permute-done.13.refs_4_) | copy-start | bytes 491524
  110.8 6.5 %collective-permute-start.15 = (bf16[128,640]{1,0:T(8,128)(2,1)S(1)}, bf16[128,640]{1,0:T(8,128)(2,1)S(1)}, u32[]{:S(2)}, u32[]{:S(2)}) collective-permute-start(bf16[128,640]{1,0:T(8,128)(2,1)S(1)} %collective-permute-done.13.refs_4_), channel_id=1, source_target_pairs={{0,7},{1,0},{2,1},{3,2},{4,3},{5,4},{6,5},{7,6},{8,15},{9,8},{10,9... | collective-permute-start | bytes 491528 | tf_op jit(solution)/shard_map/ppermute | solution.py:284
  114.6 13.3 %copy-start.17 = (bf16[128,640]{1,0:T(8,128)(2,1)}, bf16[128,640]{1,0:T(8,128)(2,1)S(1)}, u32[]{:S(2)}) copy-start(bf16[128,640]{1,0:T(8,128)(2,1)S(1)} %collective-permute-done.12.refs_3_) | copy-start | bytes 491524
  114.6 6.8 %collective-permute-start.14 = (bf16[128,640]{1,0:T(8,128)(2,1)S(1)}, bf16[128,640]{1,0:T(8,128)(2,1)S(1)}, u32[]{:S(2)}, u32[]{:S(2)}) collective-permute-start(bf16[128,640]{1,0:T(8,128)(2,1)S(1)} %collective-permute-done.12.refs_3_), channel_id=1, source_target_pairs={{0,1},{1,2},{2,3},{3,4},{4,5},{5,6},{6,7},{7,0},{8,9},{9,10},{10,1... | collective-permute-start | bytes 491528 | tf_op jit(solution)/shard_map/ppermute | solution.py:284
  117.3 5.8 %collective-permute-start.17 = (bf16[64,640]{1,0:T(8,128)(2,1)S(1)}, bf16[64,640]{1,0:T(8,128)(2,1)S(1)}, u32[]{:S(2)}, u32[]{:S(2)}) collective-permute-start(bf16[64,640]{1,0:T(8,128)(2,1)S(1)} %slice.85), channel_id=1, source_target_pairs={{0,7},{1,0},{2,1},{3,2},{4,3},{5,4},{6,5},{7,6},{8,15},{9,8},{10,9... | collective-permute-start | bytes 245768 | tf_op jit(solution)/shard_map/ppermute | solution.py:284
  121.4 5.7 %collective-permute-start.16 = (bf16[64,640]{1,0:T(8,128)(2,1)S(1)}, bf16[64,640]{1,0:T(8,128)(2,1)S(1)}, u32[]{:S(2)}, u32[]{:S(2)}) collective-permute-start(bf16[64,640]{1,0:T(8,128)(2,1)S(1)} %slice.84), channel_id=1, source_target_pairs={{0,1},{1,2},{2,3},{3,4},{4,5},{5,6},{6,7},{7,0},{8,9},{9,10},{10,1... | collective-permute-start | bytes 245768 | tf_op jit(solution)/shard_map/ppermute | solution.py:284
  132.3 67.1 %copy-start.21 = (f32[2560]{0:T(1024)S(1)}, f32[2560]{0:T(1024)}, u32[]{:S(2)}) copy-start(f32[2560]{0:T(1024)} %param.24) | copy-start | bytes 30724
  159.6 44.1 %copy-start.1 = (bf16[8,192,640]{2,1,0:T(8,128)(2,1)}, bf16[8,192,640]{2,1,0:T(8,128)(2,1)S(1)}, u32[]{:S(2)}) copy-start(bf16[8,192,640]{2,1,0:T(8,128)(2,1)S(1)} %all_to_all.10) | copy-start | bytes 5898244
  159.6 39.8 %collective-permute-start.19 = (bf16[1536,640]{1,0:T(8,128)(2,1)S(1)}, bf16[1536,640]{1,0:T(8,128)(2,1)}, u32[]{:S(2)}, u32[]{:S(2)}) collective-permute-start(bf16[1536,640]{1,0:T(8,128)(2,1)S(1)} %bitcast.120), channel_id=1, source_target_pairs={{0,16},{8,24},{16,0},{24,8},{1,17},{9,25},{17,1},{25,9},{2,18},{10... | collective-permute-start | bytes 5898248 | tf_op jit(solution)/shard_map/ppermute | solution.py:287
  160.0 40.0 %collective-permute-start.18 = (bf16[1536,640]{1,0:T(8,128)(2,1)S(1)}, bf16[1536,640]{1,0:T(8,128)(2,1)}, u32[]{:S(2)}, u32[]{:S(2)}) collective-permute-start(bf16[1536,640]{1,0:T(8,128)(2,1)S(1)} %bitcast.121), channel_id=1, source_target_pairs={{0,8},{8,0},{16,24},{24,16},{1,9},{9,1},{17,25},{25,17},{2,10},{10... | collective-permute-start | bytes 5898248 | tf_op jit(solution)/shard_map/ppermute | solution.py:287
  199.4 4.3 %collective-permute-start.20 = (bf16[1536,640]{1,0:T(8,128)(2,1)}, bf16[1536,640]{1,0:T(8,128)(2,1)}, u32[]{:S(2)}, u32[]{:S(2)}) collective-permute-start(bf16[1536,640]{1,0:T(8,128)(2,1)} %collective-permute-done.19.x2), channel_id=1, source_target_pairs={{0,8},{8,0},{16,24},{24,16},{1,9},{9,1},{17,25},{25,17},{2,10},{10... | collective-permute-start | bytes 5898248 | tf_op jit(solution)/shard_map/ppermute | solution.py:287
  226.2 7.1 %collective-permute-start.21 = (bf16[2,1536,640]{2,1,0:T(8,128)(2,1)}, bf16[2,1536,640]{2,1,0:T(8,128)(2,1)S(1)}, u32[]{:S(2)}, u32[]{:S(2)}) collective-permute-start(bf16[2,1536,640]{2,1,0:T(8,128)(2,1)} %get-tuple-element.30), channel_id=1, source_target_pairs={{0,8},{8,0},{16,24},{24,16},{1,9},{9,1},{17,25},{25,17},{2,10},{10... | collective-permute-start | bytes 11796488 | tf_op jit(solution)/shard_map/ppermute | solution.py:287
  233.8 45.7 %copy-start.2 = (bf16[1536,640]{1,0:T(8,128)(2,1)S(1)}, bf16[1536,640]{1,0:T(8,128)(2,1)}, u32[]{:S(2)}) copy-start(bf16[1536,640]{1,0:T(8,128)(2,1)} %get-tuple-element.29) | copy-start | bytes 5898244
  234.3 45.2 %collective-permute-start.22 = (bf16[1536,640]{1,0:T(8,128)(2,1)S(1)}, bf16[1536,640]{1,0:T(8,128)(2,1)S(1)}, u32[]{:S(2)}, u32[]{:S(2)}) collective-permute-start(bf16[1536,640]{1,0:T(8,128)(2,1)S(1)} %fusion.1), channel_id=1, source_target_pairs={{0,16},{8,24},{16,0},{24,8},{1,17},{9,25},{17,1},{25,9},{2,18},{10... | collective-permute-start | bytes 5898248 | tf_op jit(solution)/shard_map/ppermute | solution.py:287
  317.8 4.5 %collective-permute-start.23 = (bf16[64,640]{1,0:T(8,128)(2,1)S(1)}, bf16[64,640]{1,0:T(8,128)(2,1)S(1)}, u32[]{:S(2)}, u32[]{:S(2)}) collective-permute-start(bf16[64,640]{1,0:T(8,128)(2,1)S(1)} %get-tuple-element.34), channel_id=1, source_target_pairs={{0,7},{1,0},{2,1},{3,2},{4,3},{5,4},{6,5},{7,6},{8,15},{9,8},{10,9... | collective-permute-start | bytes 245768 | tf_op jit(solution)/shard_map/ppermute | solution.py:284
  322.3 6.0 %collective-permute-start.24 = (bf16[128,640]{1,0:T(8,128)(2,1)S(1)}, bf16[128,640]{1,0:T(8,128)(2,1)S(1)}, u32[]{:S(2)}, u32[]{:S(2)}) collective-permute-start(bf16[128,640]{1,0:T(8,128)(2,1)S(1)} %fusion.12), channel_id=1, source_target_pairs={{0,7},{1,0},{2,1},{3,2},{4,3},{5,4},{6,5},{7,6},{8,15},{9,8},{10,9... | collective-permute-start | bytes 491528 | tf_op jit(solution)/shard_map/ppermute | solution.py:284
  328.4 8.1 %collective-permute-start.25 = (bf16[128,640]{1,0:T(8,128)(2,1)S(1)}, bf16[128,640]{1,0:T(8,128)(2,1)S(1)}, u32[]{:S(2)}, u32[]{:S(2)}) collective-permute-start(bf16[128,640]{1,0:T(8,128)(2,1)S(1)} %fusion.14), channel_id=1, source_target_pairs={{0,7},{1,0},{2,1},{3,2},{4,3},{5,4},{6,5},{7,6},{8,15},{9,8},{10,9... | collective-permute-start | bytes 491528 | tf_op jit(solution)/shard_map/ppermute | solution.py:284
  330.3 6.2 %collective-permute-start.27 = (bf16[64,640]{1,0:T(8,128)(2,1)S(1)}, bf16[64,640]{1,0:T(8,128)(2,1)S(1)}, u32[]{:S(2)}, u32[]{:S(2)}) collective-permute-start(bf16[64,640]{1,0:T(8,128)(2,1)S(1)} %get-tuple-element.35), channel_id=1, source_target_pairs={{0,1},{1,2},{2,3},{3,4},{4,5},{5,6},{6,7},{7,0},{8,9},{9,10},{10,1... | collective-permute-start | bytes 245768 | tf_op jit(solution)/shard_map/ppermute | solution.py:284
  336.5 8.3 %collective-permute-start.28 = (bf16[128,640]{1,0:T(8,128)(2,1)S(1)}, bf16[128,640]{1,0:T(8,128)(2,1)S(1)}, u32[]{:S(2)}, u32[]{:S(2)}) collective-permute-start(bf16[128,640]{1,0:T(8,128)(2,1)S(1)} %get-tuple-element.33), channel_id=1, source_target_pairs={{0,1},{1,2},{2,3},{3,4},{4,5},{5,6},{6,7},{7,0},{8,9},{9,10},{10,1... | collective-permute-start | bytes 491528 | tf_op jit(solution)/shard_map/ppermute | solution.py:284
  344.9 7.5 %collective-permute-start.29 = (bf16[128,640]{1,0:T(8,128)(2,1)S(1)}, bf16[128,640]{1,0:T(8,128)(2,1)S(1)}, u32[]{:S(2)}, u32[]{:S(2)}) collective-permute-start(bf16[128,640]{1,0:T(8,128)(2,1)S(1)} %fusion.8), channel_id=1, source_target_pairs={{0,1},{1,2},{2,3},{3,4},{4,5},{5,6},{6,7},{7,0},{8,9},{9,10},{10,1... | collective-permute-start | bytes 491528 | tf_op jit(solution)/shard_map/ppermute | solution.py:284
  344.9 7.6 %collective-permute-start.26 = (bf16[128,640]{1,0:T(8,128)(2,1)S(1)}, bf16[128,640]{1,0:T(8,128)(2,1)S(1)}, u32[]{:S(2)}, u32[]{:S(2)}) collective-permute-start(bf16[128,640]{1,0:T(8,128)(2,1)S(1)} %get-tuple-element.32), channel_id=1, source_target_pairs={{0,7},{1,0},{2,1},{3,2},{4,3},{5,4},{6,5},{7,6},{8,15},{9,8},{10,9... | collective-permute-start | bytes 491528 | tf_op jit(solution)/shard_map/ppermute | solution.py:284
  352.4 6.6 %collective-permute-start.30 = (bf16[128,640]{1,0:T(8,128)(2,1)S(1)}, bf16[128,640]{1,0:T(8,128)(2,1)S(1)}, u32[]{:S(2)}, u32[]{:S(2)}) collective-permute-start(bf16[128,640]{1,0:T(8,128)(2,1)S(1)} %fusion.10), channel_id=1, source_target_pairs={{0,1},{1,2},{2,3},{3,4},{4,5},{5,6},{6,7},{7,0},{8,9},{9,10},{10,1... | collective-permute-start | bytes 491528 | tf_op jit(solution)/shard_map/ppermute | solution.py:284
  (7 other events, 43.4 us)
Sparse Core Ops, SparseCore 0:
  10.6 68.0 all-gather.1
